TPU v7x, 256 devices: a whole 4x4x8 slice. The times are simulated.
256 devices in a mesh: fsdp: 16 (over y_lo, z), dp: 16 (over x, y_hi, core).
Axes of the slice: x: 4, y: 4 (y_hi: 2, y_lo: 2; y = y_hi * 2 + y_lo), z: 8, core: 2. Of those that a mesh axis runs over, the one named last changes fastest.
Arguments:
- patch_acts: bfloat16 [32768, 12288], P(('fsdp', 'dp')), may hold values from -6 to 6
- patch_slot: int32 [32768], P(('fsdp', 'dp')), may hold values from 0 to 1024, as said below
- out_grads: bfloat16 [16384, 3072], P(('fsdp', 'dp')), may hold values from -6 to 6
- latent_weight: bfloat16 [12288, 3072], P('dp', 'fsdp'), may hold values from -0.0546875 to 0.0546875
- step_size: bfloat16 [1, 3072], P(None, 'fsdp')
Outputs:
- grad_acts: bfloat16 [32768, 12288], P(('fsdp', 'dp'))
- grad_weight: float32 [12288, 3072], P('dp', 'fsdp')
- grad_step: float32 [1, 3072], P(None, 'fsdp')
Inputs may be any that keep to these rules, and one draw needn't show every extreme that they name: `patch_slot`: within each fsdp index, the used patch rows of every image owner come first in its 128 slots and carry a packed row below 1024, the others carry 1024; each packed row of the fsdp index receives exactly one patch row; in every fsdp index some image owner has all 128 slots used.
All inputs are finite; a program needn't handle non-finite values.
Results may differ from a plain program's by a relative error of at most 0.0049.
Values may be sent and summed in bfloat16 or wider, within the bound.
No kernel may reach another device: no remote copies, remote signals or barrier semaphores. Data moves between devices by JAX's collectives and lax.ppermute only.
A program may use at most 128 MiB of HBM per device.

v0:
```python
import jax
import jax.numpy as jnp
from jax import lax
from jax.sharding import PartitionSpec as P

FF_W = 12288
top_level = 7.0
wobble = 0.9
two_pi = 6.283185307179586
inv_root_two = 0.7071067811865476
inv_root_tau = 0.3989422804014327


def gelu_pair(values):
    normal_cdf = 0.5 * (1.0 + jax.scipy.special.erf(values * inv_root_two))
    density = jnp.exp(-0.5 * values * values) * inv_root_tau
    return (values * normal_cdf, normal_cdf + values * density)


def soft_quantize(weight, step):
    ratio = weight / step
    clipped = top_level * jnp.tanh(ratio / top_level)
    phase = two_pi * clipped
    quantized = clipped - wobble * jnp.sin(phase) / two_pi
    slope = (1.0 - wobble * jnp.cos(phase)) * (1.0 - clipped / top_level * (clipped / top_level))
    return (quantized, slope, ratio)


def contract_last(left, right):
    return lax.dot_general(
        left, right, (((1,), (1,)), ((), ())), preferred_element_type=jnp.float32
    )


def contract_first(left, right):
    return lax.dot_general(
        left, right, (((0,), (0,)), ((), ())), preferred_element_type=jnp.float32
    )


def shards(patch_acts, patch_slot, out_grads, latent_weight, step_size):
    dp_count = lax.axis_size("dp")
    capacity, features = patch_acts.shape
    hidden = features // dp_count
    packed_rows = out_grads.shape[0] * dp_count
    outgoing = patch_acts.reshape(capacity, dp_count, hidden)
    labels = jnp.broadcast_to(patch_slot[:, None], (capacity, dp_count))
    incoming, slot_labels = (
        lax.all_to_all(outgoing, "dp", split_axis=1, concat_axis=0, tiled=True),
        lax.all_to_all(labels, "dp", split_axis=1, concat_axis=0, tiled=True),
    )
    incoming = incoming.reshape(dp_count * capacity, hidden)
    slot_labels = slot_labels.reshape(dp_count * capacity)
    holder = jnp.zeros((packed_rows + 1, hidden), jnp.bfloat16).at[slot_labels].set(incoming)
    packed = holder[:packed_rows]
    act_full, gelu_slope = gelu_pair(packed.astype(jnp.float32))
    act = act_full.astype(jnp.bfloat16)
    full_grads = lax.all_gather(out_grads, "dp", axis=0, tiled=True)
    step_local = step_size.astype(jnp.float32)
    quantized, slope, ratio = soft_quantize(latent_weight.astype(jnp.float32), step_local)
    step_piece = lax.all_gather(step_size, "fsdp", axis=1, tiled=True).astype(jnp.float32)
    piece_quant, piece_slope, piece_ratio = soft_quantize(
        lax.all_gather(latent_weight, "fsdp", axis=1, tiled=True).astype(jnp.float32), step_piece
    )
    piece_weight = (step_piece * piece_quant).astype(jnp.bfloat16)
    columns = full_grads
    grad_hidden = contract_last(columns, piece_weight)
    grad_packed = (grad_hidden * gelu_slope).astype(jnp.bfloat16)
    padded = jnp.concatenate([grad_packed, jnp.zeros((1, hidden), jnp.bfloat16)], axis=0)
    picked = jnp.take(padded, slot_labels, axis=0).reshape(dp_count * capacity, 1, hidden)
    returned = lax.all_to_all(picked, "dp", split_axis=0, concat_axis=1, tiled=True)
    grad_acts = returned.reshape(capacity, features)
    columns = full_grads
    grad_qweight = lax.psum_scatter(
        contract_first(columns, act), "fsdp", scatter_dimension=0, tiled=True
    ).T
    grad_weight = grad_qweight * slope
    partial_step = jnp.sum(grad_qweight * (quantized - ratio * slope), axis=0, keepdims=True)
    scale_factor = (FF_W * top_level) ** (-0.5)
    grad_step = scale_factor * lax.psum(partial_step, "dp")
    return (grad_acts, grad_weight, grad_step)


def solution(mesh):
    return jax.shard_map(
        shards,
        mesh=mesh,
        in_specs=(
            P(("fsdp", "dp"), None),
            P(("fsdp", "dp")),
            P(("fsdp", "dp"), None),
            P("dp", "fsdp"),
            P(None, "fsdp"),
        ),
        out_specs=(P(("fsdp", "dp"), None), P("dp", "fsdp"), P(None, "fsdp")),
        check_vma=False,
    )
```

profile of v0, /device:TPU:8, one launch (start us, length us, event | category | flops | bytes accessed | tf_op | source)
XLA Modules:
  0.0 394.6 jit_solution(10012122353420767556)
XLA Ops:
  7.2 0.0 all-gather.5.cloned.1.call-start
  7.2 0.7 all-gather.5.cloned.1.call-update
  7.9 0.0 all-gather.3.cloned.1.call-start
  7.9 0.7 all-gather.3.cloned.1.call-update
  8.6 1.3 broadcast_in_dim.24
  9.9 6.1 %all-to-all-start = ((s32[128,16,1]{0,2,1:T(1,128)}), s32[128,16,1]{0,2,1:T(1,128)S(1)}, u32[]{:S(2)}, u32[]{:S(2)}) async-start(s32[128,16,1]{0,2,1:T(1,128)} %broadcast_in_dim.24), calls=%async_computation | async-start | bytes 16384 | tf_op jit(solution)/shard_map/all_to_all | solution.py:50
  16.1 3.5 copy.35
  19.5 2.8 copy.36
  22.3 1.2 all-to-all-done
  23.5 6.0 %all-to-all-start.1 = ((bf16[128,16,768]{2,0,1:T(8,128)(2,1)}), bf16[128,16,768]{2,0,1:T(8,128)(2,1)S(1)}, u32[]{:S(2)}, u32[]{:S(2)}) async-start(bf16[128,16,768]{2,0,1:T(8,128)(2,1)} %copy.36), calls=%async_computation.1 | async-start | bytes 6291456 | tf_op jit(solution)/shard_map/all_to_all | solution.py:49
  29.5 0.0 reduce-scatter.4.cloned.1.call-start
  29.6 50.0 %all-to-all-done.1 = bf16[128,16,768]{2,0,1:T(8,128)(2,1)S(1)} async-done(((bf16[128,16,768]{2,0,1:T(8,128)(2,1)}), bf16[128,16,768]{2,0,1:T(8,128)(2,1)S(1)}, u32[]{:S(2)}, u32[]{:S(2)}) %all-to-all-start.1) | async-done | bytes 3145760 | tf_op jit(solution)/shard_map/all_to_all | solution.py:49
  79.6 0.0 copy-start
  79.6 1.7 copy-done
  81.3 10.6 %scatter_custom_fusion = bf16[1025,768]{1,0:T(8,128)(2,1)S(1)} fusion(s32[2048]{0:T(1024)S(1)} %bitcast.43, bf16[2048,768]{1,0:T(8,128)(2,1)} %bitcast.41, bf16[]{:T(256)} %constant.16.clone.1), kind=kCustom, calls=%fused_computation.20 | custom fusion | bytes 1574912 | tf_op jit(solution)/shard_map/scatter | solution.py:54
  91.9 0.1 slice.6
  92.0 0.8 copy.47
  92.7 6.3 %all-gather.5.cloned.1.call-done = bf16[1024,3072]{1,0:T(8,128)(2,1)} async-done(((bf16[64,3072]{1,0:T(8,128)(2,1)}), bf16[1024,3072]{1,0:T(8,128)(2,1)}) %all-gather.5.cloned.1.call-update) | async-done | bytes 6291472 | tf_op jit(solution)/shard_map/all_gather | solution.py:58
  99.1 10.2 %convolution_bitcast_fusion = f32[3072,768]{0,1:T(8,128)} fusion(bf16[1024,3072]{1,0:T(8,128)(2,1)} %all-gather.5.cloned.1.call-done, bf16[1024,768]{0,1:T(8,128)(2,1)S(1)} %copy.47), kind=kOutput, calls=%fused_computation.8 | convolution fusion | flops 4836556800 | bytes 17301504 | tf_op jit(solution)/shard_map/dot_general | solution.py:36
  109.2 9.6 %copy.44 = f32[3072,768]{1,0:T(8,128)} copy(f32[3072,768]{0,1:T(8,128)} %convolution_bitcast_fusion) | data formatting | bytes 18874368
  118.9 0.0 copy-start.2
  118.9 0.0 copy-start.1
  118.9 0.0 reduce-scatter.4.cloned.1.call-update
  118.9 0.6 copy-done.2
  119.5 0.6 dynamic-slice
  120.8 0.0 copy-done.1
  120.8 0.2 dynamic-update-slice
  121.1 35.8 %all-reduce.1 = bf16[3072]{0:T(1024)(128)(2,1)S(1)} all-reduce(bf16[3072]{0:T(1024)(128)(2,1)S(1)} %dynamic-update-slice), channel_id=1, replica_groups=mesh['fsdp'=16,'dp'=16] {'fsdp'}, use_global_device_ids=true, to_apply=%add.1 | all-reduce | flops 3072 | bytes 12288
  156.9 23.6 %all-gather.3.cloned.1.call-done = bf16[768,3072]{0,1:T(8,128)(2,1)} async-done(((bf16[768,192]{0,1:T(8,128)(2,1)}), bf16[768,3072]{0,1:T(8,128)(2,1)}) %all-gather.3.cloned.1.call-update) | async-done | bytes 4718608 | tf_op jit(solution)/shard_map/all_gather | solution.py:63
  180.6 44.4 %fusion.8 = bf16[1024,768]{0,1:T(8,128)(2,1)} fusion(bf16[1024,768]{0,1:T(8,128)(2,1)S(1)} %copy.47, bf16[1024,3072]{1,0:T(8,128)(2,1)} %all-gather.5.cloned.1.call-done, bf16[768,3072]{0,1:T(8,128)(2,1)} %all-gather.3.cloned.1.call-done, f32[3072]{0:T(1024)S(1)} %mul.123), kind=kOutput, calls=%fused_computation.17 | convolution fusion | flops 4861722624 | bytes 14168064 | tf_op jit(solution)/shard_map/dot_general | solution.py:30
  225.0 1.7 copy.48
  226.7 0.1 concatenate.3.clone
  226.8 9.4 %gather_fusion = bf16[2048,768]{1,0:T(8,128)(2,1)} fusion(bf16[1025,768]{1,0:T(8,128)(2,1)S(1)} %concatenate.3.clone, s32[2048]{0:T(1024)S(1)} %broadcast_clamp_fusion), kind=kCustom, calls=%fused_computation | custom fusion | bytes 6299648 | tf_op jit(solution)/shard_map/jit(_take)/gather | solution.py:70
  236.2 2.2 bitcast_select_fusion
  238.4 0.5 broadcast.113
  238.9 3.7 reduce.2
  242.6 6.4 %reshape.124 = bf16[16,2,49152]{2,1,0:T(2,128)(2,1)} reshape(bf16[2048,768]{1,0:T(8,128)(2,1)} %reduce.2) | data formatting | bytes 6291456
  249.0 5.9 %all-to-all-start.2 = ((bf16[16,2,49152]{2,1,0:T(2,128)(2,1)}), bf16[16,2,49152]{2,1,0:T(2,128)(2,1)S(1)}, u32[]{:S(2)}, u32[]{:S(2)}) async-start(bf16[16,2,49152]{2,1,0:T(2,128)(2,1)} %reshape.124), calls=%async_computation.2 | async-start | bytes 6291456 | tf_op jit(solution)/shard_map/all_to_all | solution.py:71
  254.9 1.1 copy.41
  256.1 70.4 %all-to-all-done.2 = bf16[16,2,49152]{2,1,0:T(2,128)(2,1)S(1)} async-done(((bf16[16,2,49152]{2,1,0:T(2,128)(2,1)}), bf16[16,2,49152]{2,1,0:T(2,128)(2,1)S(1)}, u32[]{:S(2)}, u32[]{:S(2)}) %all-to-all-start.2) | async-done | bytes 3145760 | tf_op jit(solution)/shard_map/all_to_all | solution.py:71
  326.4 7.7 %reshape.125 = bf16[2048,1,768]{2,1,0:T(2,128)(2,1)} reshape(bf16[16,2,49152]{2,1,0:T(2,128)(2,1)S(1)} %all-to-all-done.2) | data formatting | bytes 6291456
  334.1 5.0 %copy.46 = bf16[2048,1,768]{2,0,1:T(8,128)(2,1)} copy(bf16[2048,1,768]{2,1,0:T(2,128)(2,1)} %reshape.125) | data formatting | bytes 6291456
  339.1 3.5 copy.40
  342.6 2.8 copy.42
  345.4 0.0 reduce-scatter.4.cloned.1.call-done
  345.4 1.3 copy.45
  346.7 3.3 fusion.13
  350.0 1.1 copy.43
  351.1 36.4 %psum.7 = f32[1,192]{1,0:T(1,128)S(1)} all-reduce(f32[1,192]{1,0:T(1,128)S(1)} %bitcast.46), channel_id=1, replica_groups=mesh['fsdp'=16,'dp'=16] {'dp'}, use_global_device_ids=true, to_apply=%region_3.4 | all-reduce | flops 192 | bytes 1536 | tf_op jit(solution)/shard_map/psum | solution.py:80
  387.5 0.6 broadcast_multiply_fusion
  (6 shorter events, 0.1 us)
Async XLA Ops:
  7.2 91.9 %all-gather.5.cloned.1.call-start = ((), (), s32[]{:S(2)}) async-start(), calls=%async_computation.5 | async-start | bytes 6684672 | tf_op jit(solution)/shard_map/all_gather | solution.py:58
  7.9 172.7 %all-gather.3.cloned.1.call-start = ((), (), s32[]{:S(2)}) async-start(), calls=%async_computation.4 | async-start | bytes 5013504 | tf_op jit(solution)/shard_map/all_gather | solution.py:63
  9.9 13.6 %all-to-all-start = ((s32[128,16,1]{0,2,1:T(1,128)}), s32[128,16,1]{0,2,1:T(1,128)S(1)}, u32[]{:S(2)}, u32[]{:S(2)}) async-start(s32[128,16,1]{0,2,1:T(1,128)} %broadcast_in_dim.24), calls=%async_computation | async-start | bytes 16384 | tf_op jit(solution)/shard_map/all_to_all | solution.py:50
  23.5 56.1 %all-to-all-start.1 = ((bf16[128,16,768]{2,0,1:T(8,128)(2,1)}), bf16[128,16,768]{2,0,1:T(8,128)(2,1)S(1)}, u32[]{:S(2)}, u32[]{:S(2)}) async-start(bf16[128,16,768]{2,0,1:T(8,128)(2,1)} %copy.36), calls=%async_computation.1 | async-start | bytes 6291456 | tf_op jit(solution)/shard_map/all_to_all | solution.py:49
  29.5 315.8 %reduce-scatter.4.cloned.1.call-start = ((), (), s32[]{:S(2)}) async-start(), calls=%async_computation.6 | async-start | bytes 10027008
  79.6 1.7 copy-start
  118.9 0.7 copy-start.2
  118.9 1.9 copy-start.1
  249.0 77.5 %all-to-all-start.2 = ((bf16[16,2,49152]{2,1,0:T(2,128)(2,1)}), bf16[16,2,49152]{2,1,0:T(2,128)(2,1)S(1)}, u32[]{:S(2)}, u32[]{:S(2)}) async-start(bf16[16,2,49152]{2,1,0:T(2,128)(2,1)} %reshape.124), calls=%async_computation.2 | async-start | bytes 6291456 | tf_op jit(solution)/shard_map/all_to_all | solution.py:71
Sparse Core Ops, SparseCore 0:
  10.7 88.3 all-gather.4
  100.8 79.6 all-gather.2
  183.1 130.3 reduce-scatter.3
where the time goes:
time: 395 us
  waiting for transfers between devices  153 us (39%)
  local copies, waits for them, and re-layouts  72.3 us (18%)
  blocking collectives  72.2 us (18%)
  matrix products  54.6 us (14%)
  starting transfers between devices  18.2 us (5%)
  between operations  14.6 us (4%)
  other arithmetic  9.8 us (2%)
    all_to_all x1, waiting for transfers between devices, shards(): lax.all_to_all(picked, 'dp', split_axis=0, concat_axis=1, tiled=True)  70.4 us
    all_to_all x1, waiting for transfers between devices, shards(): lax.all_to_all(outgoing, 'dp', split_axis=1, concat_axis=0, tiled=True)  50 us
    dot_general x1, matrix products, contract_last(): lax.dot_general(left, right, (((1,), (1,)), ((), ())), preferred_element_...  44.4 us
    unnamed x20, local copies, waits for them, and re-layouts  44.1 us
    psum x1, blocking collectives, shards(): grad_step = scale_factor * lax.psum(partial_step, 'dp')  36.4 us
    unnamed x1, blocking collectives  35.8 us
    all_gather x1, waiting for transfers between devices, shards(): lax.all_gather(latent_weight, 'fsdp', axis=1, tiled=True)  23.6 us
    scatter x1, local copies, waits for them, and re-layouts, shards(): jnp.zeros((packed_rows + 1, hidden), jnp.bfloat16).at[slot_labels]  10.6 us
  transfers between devices with their start and end apart: 6, of which 5 were waited for; matrix products, arithmetic and copies ran while one was open for 32% of the time, Pallas kernels for 0%

commit v1 on v0

--- a/solution.py
+++ b/solution.py
@@ -77,7 +77,7 @@
     grad_weight = grad_qweight * slope
     partial_step = jnp.sum(grad_qweight * (quantized - ratio * slope), axis=0, keepdims=True)
     scale_factor = (FF_W * top_level) ** (-0.5)
-    grad_step = scale_factor * lax.psum(partial_step, "dp")
+    grad_step = scale_factor * jnp.sum(lax.all_gather(partial_step, "dp"), axis=0)
     return (grad_acts, grad_weight, grad_step)
 
 

time: 395 us -> 427 us (1.081)
  blocking collectives: 72.2 us -> 104 us
    unnamed x1 -> x2, blocking collectives: 35.8 us -> 104 us
    psum x1 -> x0, blocking collectives: 36.4 us -> none  [shards(): grad_step = scale_factor * lax.psum(partial_step, 'dp')]
    unnamed x20 -> x25, local copies, waits for them, and re-layouts: 44.1 us -> 44.9 us
  transfers between devices with their start and end apart: 6 -> 6, of which waited for: 5 -> 5; matrix products, arithmetic and copies ran while one was open for 32% -> 30% of each run, Pallas kernels for 0% -> 0%
where the time goes in v1:
time: 427 us; the launch traced here: 426 us
  waiting for transfers between devices  151 us (35%)
  blocking collectives  104 us (24%)
  local copies, waits for them, and re-layouts  73.2 us (17%)
  matrix products  54.6 us (13%)
  starting transfers between devices  18.6 us (4%)
  between operations  15.2 us (4%)
  other arithmetic  9.84 us (2%)
    unnamed x2, blocking collectives  104 us
    all_to_all x1, waiting for transfers between devices, shards(): lax.all_to_all(picked, 'dp', split_axis=0, concat_axis=1, tiled=True)  68.6 us
    all_to_all x1, waiting for transfers between devices, shards(): lax.all_to_all(outgoing, 'dp', split_axis=1, concat_axis=0, tiled=True)  50 us
    unnamed x25, local copies, waits for them, and re-layouts  44.9 us
    dot_general x1, matrix products, contract_last(): lax.dot_general(left, right, (((1,), (1,)), ((), ())), preferred_element_...  44.4 us
    all_gather x1, waiting for transfers between devices, shards(): lax.all_gather(latent_weight, 'fsdp', axis=1, tiled=True)  23.7 us
    scatter x1, local copies, waits for them, and re-layouts, shards(): jnp.zeros((packed_rows + 1, hidden), jnp.bfloat16).at[slot_labels]  10.6 us
    dot_general x1, matrix products, contract_first(): lax.dot_general(left, right, (((0,), (0,)), ((), ())), preferred_element_...  10.2 us
  transfers between devices with their start and end apart: 6, of which 5 were waited for; matrix products, arithmetic and copies ran while one was open for 30% of the time, Pallas kernels for 0%

profile of v1, /device:TPU:8, one launch (start us, length us, event | category | flops | bytes accessed | tf_op | source)
XLA Modules:
  0.0 426.5 jit_solution(13572323326055705115)
XLA Ops:
  7.2 0.0 all-gather.6.cloned.1.call-start
  7.2 0.7 all-gather.6.cloned.1.call-update
  7.9 0.0 all-gather.4.cloned.1.call-start
  7.9 0.7 all-gather.4.cloned.1.call-update
  8.6 1.3 broadcast_in_dim.21
  9.9 6.1 %all-to-all-start = ((s32[128,16,1]{0,2,1:T(1,128)}), s32[128,16,1]{0,2,1:T(1,128)S(1)}, u32[]{:S(2)}, u32[]{:S(2)}) async-start(s32[128,16,1]{0,2,1:T(1,128)} %broadcast_in_dim.21), calls=%async_computation | async-start | bytes 16384 | tf_op jit(solution)/shard_map/all_to_all | solution.py:50
  16.1 3.5 copy.45
  19.5 2.8 copy.46
  22.3 1.2 all-to-all-done
  23.5 6.0 %all-to-all-start.1 = ((bf16[128,16,768]{2,0,1:T(8,128)(2,1)}), bf16[128,16,768]{2,0,1:T(8,128)(2,1)S(1)}, u32[]{:S(2)}, u32[]{:S(2)}) async-start(bf16[128,16,768]{2,0,1:T(8,128)(2,1)} %copy.46), calls=%async_computation.1 | async-start | bytes 6291456 | tf_op jit(solution)/shard_map/all_to_all | solution.py:49
  29.5 0.0 reduce-scatter.4.cloned.1.call-start
  29.6 50.0 %all-to-all-done.1 = bf16[128,16,768]{2,0,1:T(8,128)(2,1)S(1)} async-done(((bf16[128,16,768]{2,0,1:T(8,128)(2,1)}), bf16[128,16,768]{2,0,1:T(8,128)(2,1)S(1)}, u32[]{:S(2)}, u32[]{:S(2)}) %all-to-all-start.1) | async-done | bytes 3145760 | tf_op jit(solution)/shard_map/all_to_all | solution.py:49
  79.6 0.0 copy-start
  79.6 1.7 copy-done
  81.3 10.6 %scatter_custom_fusion = bf16[1025,768]{1,0:T(8,128)(2,1)S(1)} fusion(s32[2048]{0:T(1024)S(1)} %bitcast.44, bf16[2048,768]{1,0:T(8,128)(2,1)} %bitcast.42, bf16[]{:T(256)} %constant.16.clone.1), kind=kCustom, calls=%fused_computation.20 | custom fusion | bytes 1574912 | tf_op jit(solution)/shard_map/scatter | solution.py:54
  91.9 0.1 slice.6
  92.0 0.8 copy.57
  92.7 6.3 %all-gather.6.cloned.1.call-done = bf16[1024,3072]{1,0:T(8,128)(2,1)} async-done(((bf16[64,3072]{1,0:T(8,128)(2,1)}), bf16[1024,3072]{1,0:T(8,128)(2,1)}) %all-gather.6.cloned.1.call-update) | async-done | bytes 6291472 | tf_op jit(solution)/shard_map/all_gather | solution.py:58
  99.1 10.2 %convolution_bitcast_fusion = f32[3072,768]{0,1:T(8,128)} fusion(bf16[1024,3072]{1,0:T(8,128)(2,1)} %all-gather.6.cloned.1.call-done, bf16[1024,768]{0,1:T(8,128)(2,1)S(1)} %copy.57), kind=kOutput, calls=%fused_computation.8 | convolution fusion | flops 4836556800 | bytes 17301504 | tf_op jit(solution)/shard_map/dot_general | solution.py:36
  109.2 9.6 %copy.54 = f32[3072,768]{1,0:T(8,128)} copy(f32[3072,768]{0,1:T(8,128)} %convolution_bitcast_fusion) | data formatting | bytes 18874368
  118.9 0.0 copy-start.3
  118.9 0.0 copy-start.1
  118.9 0.0 reduce-scatter.4.cloned.1.call-update
  118.9 0.6 copy-done.3
  119.5 0.6 dynamic-slice
  120.8 0.0 copy-done.1
  120.8 0.2 dynamic-update-slice
  121.1 35.8 %all-reduce.1 = bf16[3072]{0:T(1024)(128)(2,1)S(1)} all-reduce(bf16[3072]{0:T(1024)(128)(2,1)S(1)} %dynamic-update-slice), channel_id=1, replica_groups=mesh['fsdp'=16,'dp'=16] {'fsdp'}, use_global_device_ids=true, to_apply=%add.1 | all-reduce | flops 3072 | bytes 12288
  157.0 23.7 %all-gather.4.cloned.1.call-done = bf16[768,3072]{0,1:T(8,128)(2,1)} async-done(((bf16[768,192]{0,1:T(8,128)(2,1)}), bf16[768,3072]{0,1:T(8,128)(2,1)}) %all-gather.4.cloned.1.call-update) | async-done | bytes 4718608 | tf_op jit(solution)/shard_map/all_gather | solution.py:63
  180.6 44.4 %fusion.8 = bf16[1024,768]{0,1:T(8,128)(2,1)} fusion(bf16[1024,768]{0,1:T(8,128)(2,1)S(1)} %copy.57, bf16[1024,3072]{1,0:T(8,128)(2,1)} %all-gather.6.cloned.1.call-done, bf16[768,3072]{0,1:T(8,128)(2,1)} %all-gather.4.cloned.1.call-done, f32[3072]{0:T(1024)S(1)} %mul.135), kind=kOutput, calls=%fused_computation.17 | convolution fusion | flops 4861722624 | bytes 14168064 | tf_op jit(solution)/shard_map/dot_general | solution.py:30
  225.0 1.7 copy.58
  226.8 0.1 concatenate.3.clone
  226.9 9.4 %gather_fusion = bf16[2048,768]{1,0:T(8,128)(2,1)} fusion(bf16[1025,768]{1,0:T(8,128)(2,1)S(1)} %concatenate.3.clone, s32[2048]{0:T(1024)S(1)} %broadcast_clamp_fusion), kind=kCustom, calls=%fused_computation | custom fusion | bytes 6299648 | tf_op jit(solution)/shard_map/jit(_take)/gather | solution.py:70
  236.3 2.2 bitcast_select_fusion
  238.5 0.5 broadcast.124
  239.0 3.7 reduce.4
  242.7 6.4 %reshape.142 = bf16[16,2,49152]{2,1,0:T(2,128)(2,1)} reshape(bf16[2048,768]{1,0:T(8,128)(2,1)} %reduce.4) | data formatting | bytes 6291456
  249.0 0.0 copy-start.2
  249.0 6.3 %all-to-all-start.2 = ((bf16[16,2,49152]{2,1,0:T(2,128)(2,1)}), bf16[16,2,49152]{2,1,0:T(2,128)(2,1)S(1)}, u32[]{:S(2)}, u32[]{:S(2)}) async-start(bf16[16,2,49152]{2,1,0:T(2,128)(2,1)} %reshape.142), calls=%async_computation.2 | async-start | bytes 6291456 | tf_op jit(solution)/shard_map/all_to_all | solution.py:71
  255.4 1.1 copy.51
  256.5 0.0 copy-done.2
  256.5 0.6 dynamic-slice.1
  257.8 68.6 %all-to-all-done.2 = bf16[16,2,49152]{2,1,0:T(2,128)(2,1)S(1)} async-done(((bf16[16,2,49152]{2,1,0:T(2,128)(2,1)}), bf16[16,2,49152]{2,1,0:T(2,128)(2,1)S(1)}, u32[]{:S(2)}, u32[]{:S(2)}) %all-to-all-start.2) | async-done | bytes 3145760 | tf_op jit(solution)/shard_map/all_to_all | solution.py:71
  326.4 7.6 %reshape.143 = bf16[2048,1,768]{2,1,0:T(2,128)(2,1)} reshape(bf16[16,2,49152]{2,1,0:T(2,128)(2,1)S(1)} %all-to-all-done.2) | data formatting | bytes 6291456
  334.1 5.0 %copy.56 = bf16[2048,1,768]{2,0,1:T(8,128)(2,1)} copy(bf16[2048,1,768]{2,1,0:T(2,128)(2,1)} %reshape.143) | data formatting | bytes 6291456
  339.0 3.5 copy.50
  342.5 2.8 copy.52
  345.3 0.0 reduce-scatter.4.cloned.1.call-done
  345.3 1.3 copy.55
  346.6 3.3 fusion.13
  349.9 0.3 dynamic-update-slice.1
  350.2 68.0 %all-reduce.2 = f32[3072]{0:T(1024)S(1)} all-reduce(f32[3072]{0:T(1024)S(1)} %dynamic-update-slice.1), channel_id=2, replica_groups=mesh['fsdp'=16,'dp'=16] {'dp'}, use_global_device_ids=true, to_apply=%add.2 | all-reduce | flops 3072 | bytes 24576
  418.2 0.1 reshape.123
  418.3 0.6 broadcast_multiply_fusion
  418.9 1.1 copy.53
  (8 shorter events, 0.1 us)
Async XLA Ops:
  7.2 91.9 %all-gather.6.cloned.1.call-start = ((), (), s32[]{:S(2)}) async-start(), calls=%async_computation.5 | async-start | bytes 6684672 | tf_op jit(solution)/shard_map/all_gather | solution.py:58
  7.9 172.7 %all-gather.4.cloned.1.call-start = ((), (), s32[]{:S(2)}) async-start(), calls=%async_computation.4 | async-start | bytes 5013504 | tf_op jit(solution)/shard_map/all_gather | solution.py:63
  9.9 13.6 %all-to-all-start = ((s32[128,16,1]{0,2,1:T(1,128)}), s32[128,16,1]{0,2,1:T(1,128)S(1)}, u32[]{:S(2)}, u32[]{:S(2)}) async-start(s32[128,16,1]{0,2,1:T(1,128)} %broadcast_in_dim.21), calls=%async_computation | async-start | bytes 16384 | tf_op jit(solution)/shard_map/all_to_all | solution.py:50
  23.5 56.1 %all-to-all-start.1 = ((bf16[128,16,768]{2,0,1:T(8,128)(2,1)}), bf16[128,16,768]{2,0,1:T(8,128)(2,1)S(1)}, u32[]{:S(2)}, u32[]{:S(2)}) async-start(bf16[128,16,768]{2,0,1:T(8,128)(2,1)} %copy.46), calls=%async_computation.1 | async-start | bytes 6291456 | tf_op jit(solution)/shard_map/all_to_all | solution.py:49
  29.5 315.7 %reduce-scatter.4.cloned.1.call-start = ((), (), s32[]{:S(2)}) async-start(), calls=%async_computation.6 | async-start | bytes 10027008
  79.6 1.7 copy-start
  118.9 0.7 copy-start.3
  118.9 1.9 copy-start.1
  249.0 7.5 %copy-start.2 = (u32[256]{0:T(256)S(1)}, u32[256]{0:T(256)}, u32[]{:S(2)}) copy-start(u32[256]{0:T(256)} %constant.69) | copy-start | bytes 3076
  249.0 77.4 %all-to-all-start.2 = ((bf16[16,2,49152]{2,1,0:T(2,128)(2,1)}), bf16[16,2,49152]{2,1,0:T(2,128)(2,1)S(1)}, u32[]{:S(2)}, u32[]{:S(2)}) async-start(bf16[16,2,49152]{2,1,0:T(2,128)(2,1)} %reshape.142), calls=%async_computation.2 | async-start | bytes 6291456 | tf_op jit(solution)/shard_map/all_to_all | solution.py:71
Sparse Core Ops, SparseCore 0:
  10.7 88.3 all-gather.5
  100.8 79.7 all-gather.3
  183.2 130.2 reduce-scatter.3
